TPU v7x, 32 devices: a whole 2x2x4 slice. The times are simulated.
32 devices in a mesh: row: 16 (over z, x, core), col: 2 (over y).
Axes of the slice: x: 2, y: 2, z: 4, core: 2. Of those that a mesh axis runs over, the one named last changes fastest.
Arguments:
- features: bfloat16 [16384, 256], P(('row', 'col')), may hold values from -6 to 6
- grad_out: bfloat16 [16384, 256], P(('row', 'col')), may hold values from -6 to 6
- weight: bfloat16 [256, 256], replicated, may hold values from -0.375 to 0.375
- tiles: bfloat16 [6144, 128, 128], P(('row', 'col')), may hold values from -0.125 to 0.125
- tile_row: int32 [6144], P(('row', 'col')), may hold values from 0 to 7
- tile_col: int32 [6144], P(('row', 'col')), may hold values from 0 to 63
- tile_count: int32 [32], P(('row', 'col')), may hold values from 24 to 192, as said below
Outputs:
- grad_features: bfloat16 [16384, 256], P(('row', 'col'))
- grad_weight: float32 [256, 256], replicated
Inputs may be any that keep to these rules, and one draw needn't show every extreme that they name: `tile_count`: exactly 192 on some device in every draw; slots of a device from its count on are not part of the adjacency.
All inputs are finite; a program needn't handle non-finite values.
Results may differ from a plain program's by a relative error of at most 0.02.
Values may be sent and summed in bfloat16 or wider, within the bound.
A program may use at most 128 MiB of HBM per device.

v0:
```python
import jax
import jax.numpy as jnp
from jax import lax
from jax.sharding import PartitionSpec as P


def silu_grad(preact, upstream):
    sigmoid_z = jax.nn.sigmoid(preact)
    return (upstream.astype(jnp.float32) * sigmoid_z * (1.0 + preact * (1.0 - sigmoid_z))).astype(
        jnp.bfloat16
    )


def spread_tiles(tiles, read_ids, write_ids, live_mask, panel, out_tiles, transpose):
    tile_size = tiles.shape[1]
    feat_width = panel.shape[-1]
    slots = tiles.shape[0]
    shaped = (
        tiles.reshape(4, slots // 4, tile_size, tile_size),
        read_ids.reshape(4, slots // 4),
        write_ids.reshape(4, slots // 4),
        live_mask.reshape(4, slots // 4),
    )
    form = "sji,sjf->sif" if transpose else "sij,sjf->sif"

    def step(total, block_data):
        part_tiles, read_part, write_part, live_part = block_data
        picked = panel[read_part]
        product = jnp.einsum(form, part_tiles, picked, preferred_element_type=jnp.float32)
        product = product * live_part.astype(jnp.float32)[:, None, None]
        return (total.at[write_part].add(product), None)

    start = jnp.zeros((out_tiles, tile_size, feat_width), jnp.float32)
    return lax.scan(step, start, shaped)[0]


def body(features, grad_out, weight, tiles, tile_row, tile_col, tile_count):
    segment = features.shape[0]
    feat_width = features.shape[1]
    tile_size = tiles.shape[1]
    mixed_rows = jnp.dot(features, weight, preferred_element_type=jnp.float32).astype(jnp.bfloat16)
    panel = lax.all_gather(mixed_rows, "row", axis=0, tiled=True)
    live_mask = jnp.arange(tile_row.shape[0], dtype=jnp.int32) < tile_count[0]
    col_tiles = panel.shape[0] // tile_size
    row_tiles = segment * lax.axis_size("col") // tile_size
    partial_value = spread_tiles(
        tiles,
        tile_col,
        tile_row,
        live_mask,
        panel.reshape(col_tiles, tile_size, feat_width),
        row_tiles,
        False,
    )
    partial_value = partial_value.reshape(row_tiles * tile_size, feat_width)
    owned = lax.psum_scatter(
        partial_value.astype(jnp.bfloat16), "col", scatter_dimension=0, tiled=True
    ).astype(jnp.float32)
    grad_block = lax.all_gather(silu_grad(owned, grad_out), "col", axis=0, tiled=True)
    back_terms = spread_tiles(
        tiles,
        tile_row,
        tile_col,
        live_mask,
        grad_block.reshape(row_tiles, tile_size, feat_width),
        col_tiles,
        True,
    )
    back_terms = back_terms.reshape(col_tiles * tile_size, feat_width).astype(jnp.bfloat16)
    summed = lax.psum_scatter(back_terms, "row", scatter_dimension=0, tiled=True).astype(
        jnp.float32
    )
    grad_panel = summed.astype(jnp.bfloat16)
    grad_features = lax.dot_general(
        grad_panel, weight, (((1,), (1,)), ((), ())), preferred_element_type=jnp.float32
    ).astype(jnp.bfloat16)
    local_weight = lax.dot_general(
        features, grad_panel, (((0,), (0,)), ((), ())), preferred_element_type=jnp.float32
    )
    grad_weight = lax.psum(local_weight, ("row", "col"))
    return (grad_features, grad_weight)


def solution(mesh):
    in_specs = (
        P(("row", "col"), None),
        P(("row", "col"), None),
        P(),
        P(("row", "col"), None, None),
        P(("row", "col")),
        P(("row", "col")),
        P(("row", "col")),
    )
    out_specs = (P(("row", "col"), None), P())
    return jax.shard_map(body, mesh=mesh, in_specs=in_specs, out_specs=out_specs, check_vma=False)
```

profile of v0, /device:TPU:0, one launch (start us, length us, event | category | flops | bytes accessed | tf_op | source)
XLA Modules:
  0.0 485.1 jit_solution(7939529680788866499)
XLA Ops:
  7.2 0.0 copy-start
  7.2 0.0 all-gather.2.cloned.1.call-start
  7.2 0.9 copy-done
  8.1 1.8 convolution_convert_fusion.1
  9.9 0.0 all-gather.2.cloned.1.call-update
  10.0 0.0 reduce-scatter.3.cloned.1.call-start
  10.7 0.8 reshape.157
  11.4 0.8 reshape.155
  12.2 51.6 %all-gather.2.cloned.1.call-done = bf16[8192,256]{1,0:T(8,128)(2,1)} async-done(((bf16[512,256]{1,0:T(8,128)(2,1)}), bf16[8192,256]{1,0:T(8,128)(2,1)}) %all-gather.2.cloned.1.call-update) | async-done | bytes 4194320 | tf_op jit(solution)/shard_map/all_gather | solution.py:42
  63.8 0.1 broadcast_in_dim.8
  63.9 81.0 %while.20 = (s32[]{:T(128)}, f32[8,128,256]{2,1,0:T(8,128)S(1)}, s32[4,48]{1,0:T(4,128)S(1)}, bf16[4,48,128,128]{3,2,1,0:T(8,128)(2,1)}, s32[4,48]{1,0:T(4,128)S...) while((s32[]{:T(128)}, f32[8,128,256]{2,1,0:T(8,128)S(1)}, ...), condition=%wide.region_2.3_spmd, body=%wide.region_0.2_spmd.sunk | while | flops 405800288 | bytes 36181848 | solution.py:34
  64.0 4.8 gather_fusion
  68.8 6.0 %broadcast_multiply_fusion.4 = f32[48,128,256]{2,1,0:T(8,128)} fusion(f32[48]{0:T(128)S(1)} %fusion.41, bf16[48,128,256]{2,1,0:T(8,128)(2,1)} %gather_fusion, bf16[4,48,128,128]{3,2,1,0:T(8,128)(2,1)} %get-tuple-element.232, s32[]{:T(128)S(6)} %copy.17), kind=kOutput, calls=%fused_computation.4.clone.1 | convolution fusion | flops 404226048 | bytes 11010244 | tf_op jit(solution)/shard_map/while/body/eval_jaxpr/sij,sjf->sif/dot_general | solution.py:29
  74.8 9.4 %scatter_fusion = f32[8,128,256]{2,1,0:T(8,128)S(1)} fusion(f32[8,128,256]{2,1,0:T(8,128)S(1)} %get-tuple-element.222, s32[48]{0:T(128)S(1)} %get-tuple-element.202, f32[48,128,256]{2,1,0:T(8,128)} %broadcast_multiply_fusion.4), kind=kCustom, calls=%fused_computation.2.clone.1 | custom fusion | flops 1572864 | bytes 18874560 | tf_op jit(solution)/shard_map/while/body/eval_jaxpr/scatter-add | solution.py:31
  84.2 4.8 gather_fusion
  89.0 6.0 %broadcast_multiply_fusion.4 = f32[48,128,256]{2,1,0:T(8,128)} fusion(f32[48]{0:T(128)S(1)} %fusion.41, bf16[48,128,256]{2,1,0:T(8,128)(2,1)} %gather_fusion, bf16[4,48,128,128]{3,2,1,0:T(8,128)(2,1)} %get-tuple-element.232, s32[]{:T(128)S(6)} %copy.17), kind=kOutput, calls=%fused_computation.4.clone.1 | convolution fusion | flops 404226048 | bytes 11010244 | tf_op jit(solution)/shard_map/while/body/eval_jaxpr/sij,sjf->sif/dot_general | solution.py:29
  95.0 9.4 %scatter_fusion = f32[8,128,256]{2,1,0:T(8,128)S(1)} fusion(f32[8,128,256]{2,1,0:T(8,128)S(1)} %get-tuple-element.222, s32[48]{0:T(128)S(1)} %get-tuple-element.202, f32[48,128,256]{2,1,0:T(8,128)} %broadcast_multiply_fusion.4), kind=kCustom, calls=%fused_computation.2.clone.1 | custom fusion | flops 1572864 | bytes 18874560 | tf_op jit(solution)/shard_map/while/body/eval_jaxpr/scatter-add | solution.py:31
  104.5 4.8 gather_fusion
  109.3 6.0 %broadcast_multiply_fusion.4 = f32[48,128,256]{2,1,0:T(8,128)} fusion(f32[48]{0:T(128)S(1)} %fusion.41, bf16[48,128,256]{2,1,0:T(8,128)(2,1)} %gather_fusion, bf16[4,48,128,128]{3,2,1,0:T(8,128)(2,1)} %get-tuple-element.232, s32[]{:T(128)S(6)} %copy.17), kind=kOutput, calls=%fused_computation.4.clone.1 | convolution fusion | flops 404226048 | bytes 11010244 | tf_op jit(solution)/shard_map/while/body/eval_jaxpr/sij,sjf->sif/dot_general | solution.py:29
  115.3 9.4 %scatter_fusion = f32[8,128,256]{2,1,0:T(8,128)S(1)} fusion(f32[8,128,256]{2,1,0:T(8,128)S(1)} %get-tuple-element.222, s32[48]{0:T(128)S(1)} %get-tuple-element.202, f32[48,128,256]{2,1,0:T(8,128)} %broadcast_multiply_fusion.4), kind=kCustom, calls=%fused_computation.2.clone.1 | custom fusion | flops 1572864 | bytes 18874560 | tf_op jit(solution)/shard_map/while/body/eval_jaxpr/scatter-add | solution.py:31
  124.8 4.8 gather_fusion
  129.5 6.0 %broadcast_multiply_fusion.4 = f32[48,128,256]{2,1,0:T(8,128)} fusion(f32[48]{0:T(128)S(1)} %fusion.41, bf16[48,128,256]{2,1,0:T(8,128)(2,1)} %gather_fusion, bf16[4,48,128,128]{3,2,1,0:T(8,128)(2,1)} %get-tuple-element.232, s32[]{:T(128)S(6)} %copy.17), kind=kOutput, calls=%fused_computation.4.clone.1 | convolution fusion | flops 404226048 | bytes 11010244 | tf_op jit(solution)/shard_map/while/body/eval_jaxpr/sij,sjf->sif/dot_general | solution.py:29
  135.5 9.4 %scatter_fusion = f32[8,128,256]{2,1,0:T(8,128)S(1)} fusion(f32[8,128,256]{2,1,0:T(8,128)S(1)} %get-tuple-element.222, s32[48]{0:T(128)S(1)} %get-tuple-element.202, f32[48,128,256]{2,1,0:T(8,128)} %broadcast_multiply_fusion.4), kind=kCustom, calls=%fused_computation.2.clone.1 | custom fusion | flops 1572864 | bytes 18874560 | tf_op jit(solution)/shard_map/while/body/eval_jaxpr/scatter-add | solution.py:31
  144.9 0.9 convert_element_type.51
  145.8 0.0 reduce-scatter.3.cloned.1.call-update
  145.8 0.0 copy-start.2
  145.8 0.0 reduce-scatter.5.cloned.1.call-start
  145.9 8.7 %copy.9 = bf16[192,128,128]{1,2,0:T(8,128)(2,1)} copy(bf16[192,128,128]{2,1,0:T(8,128)(2,1)} %bitcast.83) | data formatting | bytes 12582912 | tf_op args[3]
  154.6 4.6 reduce-scatter.3.cloned.1.call-done
  159.1 0.0 copy-done.2
  159.1 1.2 fusion.21
  160.3 8.6 %all_gather.7 = bf16[1024,256]{1,0:T(8,128)(2,1)S(1)} all-gather(bf16[512,256]{1,0:T(8,128)(2,1)S(1)} %fusion.21), channel_id=1, replica_groups=mesh['row'=16,'col'=2] {'col'}, dimensions={0}, use_global_device_ids=true | all-gather | bytes 786432 | tf_op jit(solution)/shard_map/all_gather | solution.py:59
  168.9 4.2 broadcast_in_dim.4
  173.1 93.3 %while.21 = (s32[]{:T(128)}, f32[64,128,256]{2,1,0:T(8,128)}, s32[4,48]{1,0:T(4,128)S(1)}, bf16[4,48,128,128]{2,3,1,0:T(8,128)(2,1)}, s32[4,48]{1,0:T(4,128)S(1)...) while((s32[]{:T(128)}, f32[64,128,256]{2,1,0:T(8,128)}, ...), condition=%wide.region_6.7_spmd, body=%wide.region_4.6_spmd.sunk | while | flops 405800288 | bytes 36181848 | solution.py:34
  173.1 2.5 gather_fusion.1
  175.7 5.9 %broadcast_multiply_fusion.5 = f32[48,128,256]{2,1,0:T(8,128)} fusion(f32[48]{0:T(128)S(1)} %fusion.45, bf16[48,128,256]{2,1,0:T(8,128)(2,1)} %gather_fusion.1, bf16[4,48,128,128]{2,3,1,0:T(8,128)(2,1)} %get-tuple-element.256, s32[]{:T(128)S(6)} %copy.23), kind=kOutput, calls=%fused_computation.19.clone.1 | convolution fusion | flops 404226048 | bytes 11010244 | tf_op jit(solution)/shard_map/while/body/eval_jaxpr/sji,sjf->sif/dot_general | solution.py:29
  181.6 14.8 %scatter_fusion.1 = f32[64,128,256]{2,1,0:T(8,128)} fusion(f32[64,128,256]{2,1,0:T(8,128)} %get-tuple-element.246, s32[48]{0:T(128)S(1)} %get-tuple-element.211, f32[48,128,256]{2,1,0:T(8,128)} %broadcast_multiply_fusion.5), kind=kCustom, calls=%fused_computation.3.clone.1 | custom fusion | flops 1572864 | bytes 18874560 | tf_op jit(solution)/shard_map/while/body/eval_jaxpr/scatter-add | solution.py:31
  196.4 2.5 gather_fusion.1
  198.9 5.9 %broadcast_multiply_fusion.5 = f32[48,128,256]{2,1,0:T(8,128)} fusion(f32[48]{0:T(128)S(1)} %fusion.45, bf16[48,128,256]{2,1,0:T(8,128)(2,1)} %gather_fusion.1, bf16[4,48,128,128]{2,3,1,0:T(8,128)(2,1)} %get-tuple-element.256, s32[]{:T(128)S(6)} %copy.23), kind=kOutput, calls=%fused_computation.19.clone.1 | convolution fusion | flops 404226048 | bytes 11010244 | tf_op jit(solution)/shard_map/while/body/eval_jaxpr/sji,sjf->sif/dot_general | solution.py:29
  204.8 14.9 %scatter_fusion.1 = f32[64,128,256]{2,1,0:T(8,128)} fusion(f32[64,128,256]{2,1,0:T(8,128)} %get-tuple-element.246, s32[48]{0:T(128)S(1)} %get-tuple-element.211, f32[48,128,256]{2,1,0:T(8,128)} %broadcast_multiply_fusion.5), kind=kCustom, calls=%fused_computation.3.clone.1 | custom fusion | flops 1572864 | bytes 18874560 | tf_op jit(solution)/shard_map/while/body/eval_jaxpr/scatter-add | solution.py:31
  219.7 2.5 gather_fusion.1
  222.3 5.9 %broadcast_multiply_fusion.5 = f32[48,128,256]{2,1,0:T(8,128)} fusion(f32[48]{0:T(128)S(1)} %fusion.45, bf16[48,128,256]{2,1,0:T(8,128)(2,1)} %gather_fusion.1, bf16[4,48,128,128]{2,3,1,0:T(8,128)(2,1)} %get-tuple-element.256, s32[]{:T(128)S(6)} %copy.23), kind=kOutput, calls=%fused_computation.19.clone.1 | convolution fusion | flops 404226048 | bytes 11010244 | tf_op jit(solution)/shard_map/while/body/eval_jaxpr/sji,sjf->sif/dot_general | solution.py:29
  228.2 14.9 %scatter_fusion.1 = f32[64,128,256]{2,1,0:T(8,128)} fusion(f32[64,128,256]{2,1,0:T(8,128)} %get-tuple-element.246, s32[48]{0:T(128)S(1)} %get-tuple-element.211, f32[48,128,256]{2,1,0:T(8,128)} %broadcast_multiply_fusion.5), kind=kCustom, calls=%fused_computation.3.clone.1 | custom fusion | flops 1572864 | bytes 18874560 | tf_op jit(solution)/shard_map/while/body/eval_jaxpr/scatter-add | solution.py:31
  243.1 2.5 gather_fusion.1
  245.7 5.9 %broadcast_multiply_fusion.5 = f32[48,128,256]{2,1,0:T(8,128)} fusion(f32[48]{0:T(128)S(1)} %fusion.45, bf16[48,128,256]{2,1,0:T(8,128)(2,1)} %gather_fusion.1, bf16[4,48,128,128]{2,3,1,0:T(8,128)(2,1)} %get-tuple-element.256, s32[]{:T(128)S(6)} %copy.23), kind=kOutput, calls=%fused_computation.19.clone.1 | convolution fusion | flops 404226048 | bytes 11010244 | tf_op jit(solution)/shard_map/while/body/eval_jaxpr/sji,sjf->sif/dot_general | solution.py:29
  251.6 14.9 %scatter_fusion.1 = f32[64,128,256]{2,1,0:T(8,128)} fusion(f32[64,128,256]{2,1,0:T(8,128)} %get-tuple-element.246, s32[48]{0:T(128)S(1)} %get-tuple-element.211, f32[48,128,256]{2,1,0:T(8,128)} %broadcast_multiply_fusion.5), kind=kCustom, calls=%fused_computation.3.clone.1 | custom fusion | flops 1572864 | bytes 18874560 | tf_op jit(solution)/shard_map/while/body/eval_jaxpr/scatter-add | solution.py:31
  266.4 0.0 copy-start.1
  266.4 6.0 %convert_element_type.55 = bf16[64,128,256]{2,1,0:T(8,128)(2,1)} convert(f32[64,128,256]{2,1,0:T(8,128)} %get-tuple-element.77) | non-fusion elementwise | flops 2097152 | bytes 12582912 | tf_op jit(solution)/shard_map/convert_element_type | solution.py:69
  272.4 0.0 reduce-scatter.5.cloned.1.call-update
  272.4 0.0 all-reduce.2.cloned.1.call-start
  272.5 72.7 %reduce-scatter.5.cloned.1.call-done = bf16[512,256]{1,0:T(8,128)(2,1)} async-done(((bf16[8192,256]{1,0:T(8,128)(2,1)}), bf16[512,256]{1,0:T(8,128)(2,1)}) %reduce-scatter.5.cloned.1.call-update) | async-done | bytes 262160 | tf_op jit(solution)/shard_map/reduce_scatter | solution.py:70
  345.2 1.9 convolution_bitcast_fusion
  347.1 0.0 all-reduce.2.cloned.1.call-update
  347.1 0.0 copy-done.1
  347.1 1.9 convolution_convert_fusion
  349.1 127.8 %all-reduce.2.cloned.1.call-done = f32[256,256]{0,1:T(8,128)} async-done(((f32[256,256]{0,1:T(8,128)}), f32[256,256]{0,1:T(8,128)}) %all-reduce.2.cloned.1.call-update) | async-done | bytes 262160 | tf_op jit(solution)/shard_map/psum | solution.py:80
  476.8 1.8 copy.11
  (25 shorter events, 0.2 us)
Async XLA Ops:
  7.2 1.0 copy-start
  7.2 56.7 %all-gather.2.cloned.1.call-start = ((), (), s32[]{:S(2)}) async-start(), calls=%async_computation.2 | async-start | bytes 4456448 | tf_op jit(solution)/shard_map/all_gather | solution.py:42
  10.0 149.2 %reduce-scatter.3.cloned.1.call-start = ((), (), s32[]{:S(2)}) async-start(), calls=%async_computation.3 | async-start | bytes 786432 | tf_op jit(solution)/shard_map/reduce_scatter | solution.py:56
  145.8 13.3 %copy-start.2 = (bf16[512,256]{1,0:T(8,128)(2,1)S(1)}, bf16[512,256]{1,0:T(8,128)(2,1)}, u32[]{:S(2)}) copy-start(bf16[512,256]{1,0:T(8,128)(2,1)} %param.12) | copy-start | bytes 786436
  145.8 199.4 %reduce-scatter.5.cloned.1.call-start = ((), (), s32[]{:S(2)}) async-start(), calls=%async_computation.4 | async-start | bytes 4456448 | tf_op jit(solution)/shard_map/reduce_scatter | solution.py:70
  266.4 80.7 %copy-start.1 = (bf16[256,256]{1,0:T(8,128)(2,1)S(1)}, bf16[256,256]{1,0:T(8,128)(2,1)}, u32[]{:S(2)}) copy-start(bf16[256,256]{1,0:T(8,128)(2,1)} %param.13) | copy-start | bytes 393220
  272.4 204.4 %all-reduce.2.cloned.1.call-start = ((), (), s32[]{:S(2)}) async-start(), calls=%async_computation.5 | async-start | bytes 524288 | tf_op jit(solution)/shard_map/psum | solution.py:80
Sparse Core Ops, SparseCore 0:
  10.7 53.0 all-gather.1
  145.9 13.1 reduce-scatter.2
  272.6 72.5 reduce-scatter.4
  351.1 125.6 all-reduce.1
where the time goes:
time: 486 us; the launch traced here: 485 us
  waiting for transfers between devices  257 us (53%)
  other arithmetic  105 us (22%)
  matrix products  53.2 us (11%)
  local copies, waits for them, and re-layouts  46.5 us (10%)
  between operations  14.5 us (3%)
  blocking collectives  8.55 us (2%)
    psum x1, waiting for transfers between devices, body(): grad_weight = lax.psum(local_weight, ('row', 'col'))  128 us
    scatter-add x8, other arithmetic, step(): return (total.at[write_part].add(product), None)  97.1 us
    reduce_scatter x1, waiting for transfers between devices, body(): lax.psum_scatter(back_terms, 'row', scatter_dimension=0, tiled=True)  72.7 us
    all_gather x1, waiting for transfers between devices, body(): panel = lax.all_gather(mixed_rows, 'row', axis=0, tiled=True)  51.6 us
    dot_general x8, matrix products, step(): jnp.einsum(form, part_tiles, picked, preferred_element_type=jnp.float32)  47.5 us
    gather x8, local copies, waits for them, and re-layouts, step(): picked = panel[read_part]  29.3 us
    unnamed x8, local copies, waits for them, and re-layouts  11.4 us
  transfers between devices with their start and end apart: 4, of which 4 were waited for; matrix products, arithmetic and copies ran while one was open for 2% of the time, Pallas kernels for 0%

commit v1 on v0

--- a/solution.py
+++ b/solution.py
@@ -2,6 +2,8 @@
 import jax.numpy as jnp
 from jax import lax
 from jax.sharding import PartitionSpec as P
+
+wrap_ladders = lambda raw: lax.all_gather(raw, ("row", "col")).sum(axis=0)
 
 
 def silu_grad(preact, upstream):
@@ -77,7 +79,7 @@
     local_weight = lax.dot_general(
         features, grad_panel, (((0,), (0,)), ((), ())), preferred_element_type=jnp.float32
     )
-    grad_weight = lax.psum(local_weight, ("row", "col"))
+    grad_weight = wrap_ladders(local_weight)
     return (grad_features, grad_weight)
 
 

time: 486 us -> 449 us (0.924)
  waiting for transfers between devices: 257 us -> 211 us
  local copies, waits for them, and re-layouts: 46.5 us -> 52.4 us
    psum x1 -> x0, waiting for transfers between devices: 128 us -> none  [body(): grad_weight = lax.psum(local_weight, ('row', 'col'))]
    all_gather x0 -> x1, waiting for transfers between devices: none -> 82.6 us  [wrap_ladders = lambda raw: lax.all_gather(raw, ('row', 'col')).sum(axis=0)]
    unnamed x8 -> x9, local copies, waits for them, and re-layouts: 11.4 us -> 17.3 us
  transfers between devices with their start and end apart: 4 -> 4, of which waited for: 4 -> 4; matrix products, arithmetic and copies ran while one was open for 2% -> 3% of each run, Pallas kernels for 0% -> 0%
where the time goes in v1:
time: 449 us; the launch traced here: 448 us
  waiting for transfers between devices  211 us (47%)
  other arithmetic  107 us (24%)
  matrix products  53.2 us (12%)
  local copies, waits for them, and re-layouts  52.4 us (12%)
  between operations  14.5 us (3%)
  blocking collectives  8.53 us (2%)
    scatter-add x8, other arithmetic, step(): return (total.at[write_part].add(product), None)  97.1 us
    all_gather x1, waiting for transfers between devices, wrap_ladders = lambda raw: lax.all_gather(raw, ('row', 'col')).sum(axis=0)  82.6 us
    reduce_scatter x1, waiting for transfers between devices, body(): lax.psum_scatter(back_terms, 'row', scatter_dimension=0, tiled=True)  72.5 us
    all_gather x1, waiting for transfers between devices, body(): panel = lax.all_gather(mixed_rows, 'row', axis=0, tiled=True)  51.6 us
    dot_general x8, matrix products, step(): jnp.einsum(form, part_tiles, picked, preferred_element_type=jnp.float32)  47.5 us
    gather x8, local copies, waits for them, and re-layouts, step(): picked = panel[read_part]  29.3 us
    unnamed x9, local copies, waits for them, and re-layouts  17.3 us
  transfers between devices with their start and end apart: 4, of which 4 were waited for; matrix products, arithmetic and copies ran while one was open for 3% of the time, Pallas kernels for 0%

profile of v1, /device:TPU:0, one launch (start us, length us, event | category | flops | bytes accessed | tf_op | source)
XLA Modules:
  0.0 447.8 jit_solution(4752558002948924625)
XLA Ops:
  7.2 0.0 copy-start
  7.2 0.0 all-gather.4.cloned.1.call-start
  7.2 0.9 copy-done
  8.1 1.8 convolution_convert_fusion.1
  10.0 0.0 all-gather.4.cloned.1.call-update
  10.0 0.0 reduce-scatter.3.cloned.1.call-start
  10.7 0.8 reshape.157
  11.4 0.8 reshape.155
  12.2 51.6 %all-gather.4.cloned.1.call-done = bf16[8192,256]{1,0:T(8,128)(2,1)} async-done(((bf16[512,256]{1,0:T(8,128)(2,1)}), bf16[8192,256]{1,0:T(8,128)(2,1)}) %all-gather.4.cloned.1.call-update) | async-done | bytes 4194320 | tf_op jit(solution)/shard_map/all_gather | solution.py:44
  63.8 0.1 broadcast_in_dim.8
  63.9 81.0 %while.20 = (s32[]{:T(128)}, f32[8,128,256]{2,1,0:T(8,128)S(1)}, s32[4,48]{1,0:T(4,128)S(1)}, bf16[4,48,128,128]{3,2,1,0:T(8,128)(2,1)}, s32[4,48]{1,0:T(4,128)S...) while((s32[]{:T(128)}, f32[8,128,256]{2,1,0:T(8,128)S(1)}, ...), condition=%wide.region_2.3_spmd, body=%wide.region_0.2_spmd.sunk | while | flops 405800288 | bytes 36181848 | solution.py:36
  64.0 4.8 %gather_fusion = bf16[48,128,256]{2,1,0:T(8,128)(2,1)} fusion(bf16[64,128,256]{2,1,0:T(8,128)(2,1)} %get-tuple-element.241, s32[1024]{0:T(1024)S(1)} %pad_clamp_fusion.4), kind=kCustom, calls=%fused_computation.clone.1 | custom fusion | bytes 6291648 | tf_op jit(solution)/shard_map/while/body/eval_jaxpr/gather | solution.py:30
  68.8 6.0 %broadcast_multiply_fusion.4 = f32[48,128,256]{2,1,0:T(8,128)} fusion(f32[48]{0:T(128)S(1)} %fusion.41, bf16[48,128,256]{2,1,0:T(8,128)(2,1)} %gather_fusion, bf16[4,48,128,128]{3,2,1,0:T(8,128)(2,1)} %get-tuple-element.239, s32[]{:T(128)S(6)} %copy.20), kind=kOutput, calls=%fused_computation.4.clone.1 | convolution fusion | flops 404226048 | bytes 11010244 | tf_op jit(solution)/shard_map/while/body/eval_jaxpr/sij,sjf->sif/dot_general | solution.py:31
  74.8 9.4 %scatter_fusion = f32[8,128,256]{2,1,0:T(8,128)S(1)} fusion(f32[8,128,256]{2,1,0:T(8,128)S(1)} %get-tuple-element.229, s32[48]{0:T(128)S(1)} %get-tuple-element.209, f32[48,128,256]{2,1,0:T(8,128)} %broadcast_multiply_fusion.4), kind=kCustom, calls=%fused_computation.2.clone.1 | custom fusion | flops 1572864 | bytes 18874560 | tf_op jit(solution)/shard_map/while/body/eval_jaxpr/scatter-add | solution.py:33
  84.2 4.8 %gather_fusion = bf16[48,128,256]{2,1,0:T(8,128)(2,1)} fusion(bf16[64,128,256]{2,1,0:T(8,128)(2,1)} %get-tuple-element.241, s32[1024]{0:T(1024)S(1)} %pad_clamp_fusion.4), kind=kCustom, calls=%fused_computation.clone.1 | custom fusion | bytes 6291648 | tf_op jit(solution)/shard_map/while/body/eval_jaxpr/gather | solution.py:30
  89.0 6.0 %broadcast_multiply_fusion.4 = f32[48,128,256]{2,1,0:T(8,128)} fusion(f32[48]{0:T(128)S(1)} %fusion.41, bf16[48,128,256]{2,1,0:T(8,128)(2,1)} %gather_fusion, bf16[4,48,128,128]{3,2,1,0:T(8,128)(2,1)} %get-tuple-element.239, s32[]{:T(128)S(6)} %copy.20), kind=kOutput, calls=%fused_computation.4.clone.1 | convolution fusion | flops 404226048 | bytes 11010244 | tf_op jit(solution)/shard_map/while/body/eval_jaxpr/sij,sjf->sif/dot_general | solution.py:31
  95.0 9.4 %scatter_fusion = f32[8,128,256]{2,1,0:T(8,128)S(1)} fusion(f32[8,128,256]{2,1,0:T(8,128)S(1)} %get-tuple-element.229, s32[48]{0:T(128)S(1)} %get-tuple-element.209, f32[48,128,256]{2,1,0:T(8,128)} %broadcast_multiply_fusion.4), kind=kCustom, calls=%fused_computation.2.clone.1 | custom fusion | flops 1572864 | bytes 18874560 | tf_op jit(solution)/shard_map/while/body/eval_jaxpr/scatter-add | solution.py:33
  104.5 4.8 %gather_fusion = bf16[48,128,256]{2,1,0:T(8,128)(2,1)} fusion(bf16[64,128,256]{2,1,0:T(8,128)(2,1)} %get-tuple-element.241, s32[1024]{0:T(1024)S(1)} %pad_clamp_fusion.4), kind=kCustom, calls=%fused_computation.clone.1 | custom fusion | bytes 6291648 | tf_op jit(solution)/shard_map/while/body/eval_jaxpr/gather | solution.py:30
  109.3 6.0 %broadcast_multiply_fusion.4 = f32[48,128,256]{2,1,0:T(8,128)} fusion(f32[48]{0:T(128)S(1)} %fusion.41, bf16[48,128,256]{2,1,0:T(8,128)(2,1)} %gather_fusion, bf16[4,48,128,128]{3,2,1,0:T(8,128)(2,1)} %get-tuple-element.239, s32[]{:T(128)S(6)} %copy.20), kind=kOutput, calls=%fused_computation.4.clone.1 | convolution fusion | flops 404226048 | bytes 11010244 | tf_op jit(solution)/shard_map/while/body/eval_jaxpr/sij,sjf->sif/dot_general | solution.py:31
  115.3 9.4 %scatter_fusion = f32[8,128,256]{2,1,0:T(8,128)S(1)} fusion(f32[8,128,256]{2,1,0:T(8,128)S(1)} %get-tuple-element.229, s32[48]{0:T(128)S(1)} %get-tuple-element.209, f32[48,128,256]{2,1,0:T(8,128)} %broadcast_multiply_fusion.4), kind=kCustom, calls=%fused_computation.2.clone.1 | custom fusion | flops 1572864 | bytes 18874560 | tf_op jit(solution)/shard_map/while/body/eval_jaxpr/scatter-add | solution.py:33
  124.7 4.8 %gather_fusion = bf16[48,128,256]{2,1,0:T(8,128)(2,1)} fusion(bf16[64,128,256]{2,1,0:T(8,128)(2,1)} %get-tuple-element.241, s32[1024]{0:T(1024)S(1)} %pad_clamp_fusion.4), kind=kCustom, calls=%fused_computation.clone.1 | custom fusion | bytes 6291648 | tf_op jit(solution)/shard_map/while/body/eval_jaxpr/gather | solution.py:30
  129.5 6.0 %broadcast_multiply_fusion.4 = f32[48,128,256]{2,1,0:T(8,128)} fusion(f32[48]{0:T(128)S(1)} %fusion.41, bf16[48,128,256]{2,1,0:T(8,128)(2,1)} %gather_fusion, bf16[4,48,128,128]{3,2,1,0:T(8,128)(2,1)} %get-tuple-element.239, s32[]{:T(128)S(6)} %copy.20), kind=kOutput, calls=%fused_computation.4.clone.1 | convolution fusion | flops 404226048 | bytes 11010244 | tf_op jit(solution)/shard_map/while/body/eval_jaxpr/sij,sjf->sif/dot_general | solution.py:31
  135.5 9.4 %scatter_fusion = f32[8,128,256]{2,1,0:T(8,128)S(1)} fusion(f32[8,128,256]{2,1,0:T(8,128)S(1)} %get-tuple-element.229, s32[48]{0:T(128)S(1)} %get-tuple-element.209, f32[48,128,256]{2,1,0:T(8,128)} %broadcast_multiply_fusion.4), kind=kCustom, calls=%fused_computation.2.clone.1 | custom fusion | flops 1572864 | bytes 18874560 | tf_op jit(solution)/shard_map/while/body/eval_jaxpr/scatter-add | solution.py:33
  144.9 0.9 convert_element_type.51
  145.8 0.0 reduce-scatter.3.cloned.1.call-update
  145.8 0.0 copy-start.2
  145.8 0.0 reduce-scatter.5.cloned.1.call-start
  145.9 8.7 %copy.11 = bf16[192,128,128]{1,2,0:T(8,128)(2,1)} copy(bf16[192,128,128]{2,1,0:T(8,128)(2,1)} %bitcast.88) | data formatting | bytes 12582912 | tf_op args[3]
  154.6 4.6 %reduce-scatter.3.cloned.1.call-done = bf16[512,256]{1,0:T(8,128)(2,1)} async-done(((bf16[1024,256]{1,0:T(8,128)(2,1)}), bf16[512,256]{1,0:T(8,128)(2,1)}) %reduce-scatter.3.cloned.1.call-update) | async-done | bytes 262160 | tf_op jit(solution)/shard_map/reduce_scatter | solution.py:58
  159.1 0.0 copy-done.2
  159.1 1.2 fusion.21
  160.3 8.5 %all_gather.13 = bf16[1024,256]{1,0:T(8,128)(2,1)S(1)} all-gather(bf16[512,256]{1,0:T(8,128)(2,1)S(1)} %fusion.21), channel_id=1, replica_groups=mesh['row'=16,'col'=2] {'col'}, dimensions={0}, use_global_device_ids=true | all-gather | bytes 786432 | tf_op jit(solution)/shard_map/all_gather | solution.py:61
  168.8 4.2 broadcast_in_dim.4
  173.1 93.3 %while.21 = (s32[]{:T(128)}, f32[64,128,256]{2,1,0:T(8,128)}, s32[4,48]{1,0:T(4,128)S(1)}, bf16[4,48,128,128]{2,3,1,0:T(8,128)(2,1)}, s32[4,48]{1,0:T(4,128)S(1)...) while((s32[]{:T(128)}, f32[64,128,256]{2,1,0:T(8,128)}, ...), condition=%wide.region_6.7_spmd, body=%wide.region_4.6_spmd.sunk | while | flops 405800288 | bytes 36181848 | solution.py:36
  173.1 2.5 gather_fusion.1
  175.7 5.9 %broadcast_multiply_fusion.5 = f32[48,128,256]{2,1,0:T(8,128)} fusion(f32[48]{0:T(128)S(1)} %fusion.45, bf16[48,128,256]{2,1,0:T(8,128)(2,1)} %gather_fusion.1, bf16[4,48,128,128]{2,3,1,0:T(8,128)(2,1)} %get-tuple-element.263, s32[]{:T(128)S(6)} %copy.26), kind=kOutput, calls=%fused_computation.19.clone.1 | convolution fusion | flops 404226048 | bytes 11010244 | tf_op jit(solution)/shard_map/while/body/eval_jaxpr/sji,sjf->sif/dot_general | solution.py:31
  181.6 14.8 %scatter_fusion.1 = f32[64,128,256]{2,1,0:T(8,128)} fusion(f32[64,128,256]{2,1,0:T(8,128)} %get-tuple-element.253, s32[48]{0:T(128)S(1)} %get-tuple-element.218, f32[48,128,256]{2,1,0:T(8,128)} %broadcast_multiply_fusion.5), kind=kCustom, calls=%fused_computation.3.clone.1 | custom fusion | flops 1572864 | bytes 18874560 | tf_op jit(solution)/shard_map/while/body/eval_jaxpr/scatter-add | solution.py:33
  196.4 2.5 gather_fusion.1
  198.9 5.9 %broadcast_multiply_fusion.5 = f32[48,128,256]{2,1,0:T(8,128)} fusion(f32[48]{0:T(128)S(1)} %fusion.45, bf16[48,128,256]{2,1,0:T(8,128)(2,1)} %gather_fusion.1, bf16[4,48,128,128]{2,3,1,0:T(8,128)(2,1)} %get-tuple-element.263, s32[]{:T(128)S(6)} %copy.26), kind=kOutput, calls=%fused_computation.19.clone.1 | convolution fusion | flops 404226048 | bytes 11010244 | tf_op jit(solution)/shard_map/while/body/eval_jaxpr/sji,sjf->sif/dot_general | solution.py:31
  204.8 14.9 %scatter_fusion.1 = f32[64,128,256]{2,1,0:T(8,128)} fusion(f32[64,128,256]{2,1,0:T(8,128)} %get-tuple-element.253, s32[48]{0:T(128)S(1)} %get-tuple-element.218, f32[48,128,256]{2,1,0:T(8,128)} %broadcast_multiply_fusion.5), kind=kCustom, calls=%fused_computation.3.clone.1 | custom fusion | flops 1572864 | bytes 18874560 | tf_op jit(solution)/shard_map/while/body/eval_jaxpr/scatter-add | solution.py:33
  219.7 2.5 gather_fusion.1
  222.3 5.9 %broadcast_multiply_fusion.5 = f32[48,128,256]{2,1,0:T(8,128)} fusion(f32[48]{0:T(128)S(1)} %fusion.45, bf16[48,128,256]{2,1,0:T(8,128)(2,1)} %gather_fusion.1, bf16[4,48,128,128]{2,3,1,0:T(8,128)(2,1)} %get-tuple-element.263, s32[]{:T(128)S(6)} %copy.26), kind=kOutput, calls=%fused_computation.19.clone.1 | convolution fusion | flops 404226048 | bytes 11010244 | tf_op jit(solution)/shard_map/while/body/eval_jaxpr/sji,sjf->sif/dot_general | solution.py:31
  228.2 14.9 %scatter_fusion.1 = f32[64,128,256]{2,1,0:T(8,128)} fusion(f32[64,128,256]{2,1,0:T(8,128)} %get-tuple-element.253, s32[48]{0:T(128)S(1)} %get-tuple-element.218, f32[48,128,256]{2,1,0:T(8,128)} %broadcast_multiply_fusion.5), kind=kCustom, calls=%fused_computation.3.clone.1 | custom fusion | flops 1572864 | bytes 18874560 | tf_op jit(solution)/shard_map/while/body/eval_jaxpr/scatter-add | solution.py:33
  243.1 2.5 gather_fusion.1
  245.6 5.9 %broadcast_multiply_fusion.5 = f32[48,128,256]{2,1,0:T(8,128)} fusion(f32[48]{0:T(128)S(1)} %fusion.45, bf16[48,128,256]{2,1,0:T(8,128)(2,1)} %gather_fusion.1, bf16[4,48,128,128]{2,3,1,0:T(8,128)(2,1)} %get-tuple-element.263, s32[]{:T(128)S(6)} %copy.26), kind=kOutput, calls=%fused_computation.19.clone.1 | convolution fusion | flops 404226048 | bytes 11010244 | tf_op jit(solution)/shard_map/while/body/eval_jaxpr/sji,sjf->sif/dot_general | solution.py:31
  251.5 14.9 %scatter_fusion.1 = f32[64,128,256]{2,1,0:T(8,128)} fusion(f32[64,128,256]{2,1,0:T(8,128)} %get-tuple-element.253, s32[48]{0:T(128)S(1)} %get-tuple-element.218, f32[48,128,256]{2,1,0:T(8,128)} %broadcast_multiply_fusion.5), kind=kCustom, calls=%fused_computation.3.clone.1 | custom fusion | flops 1572864 | bytes 18874560 | tf_op jit(solution)/shard_map/while/body/eval_jaxpr/scatter-add | solution.py:33
  266.4 0.0 copy-start.1
  266.4 6.0 %convert_element_type.55 = bf16[64,128,256]{2,1,0:T(8,128)(2,1)} convert(f32[64,128,256]{2,1,0:T(8,128)} %get-tuple-element.77) | non-fusion elementwise | flops 2097152 | bytes 12582912 | tf_op jit(solution)/shard_map/convert_element_type | solution.py:71
  272.4 0.0 reduce-scatter.5.cloned.1.call-update
  272.4 0.2 all-gather.6.cloned.1.call-start
  272.6 72.5 %reduce-scatter.5.cloned.1.call-done = bf16[512,256]{1,0:T(8,128)(2,1)} async-done(((bf16[8192,256]{1,0:T(8,128)(2,1)}), bf16[512,256]{1,0:T(8,128)(2,1)}) %reduce-scatter.5.cloned.1.call-update) | async-done | bytes 262160 | tf_op jit(solution)/shard_map/reduce_scatter | solution.py:72
  345.2 1.9 convolution_bitcast_fusion
  347.1 0.0 all-gather.6.cloned.1.call-update
  347.1 0.0 copy-done.1
  347.1 1.9 convolution_convert_fusion
  349.1 82.6 %all-gather.6.cloned.1.call-done = f32[8192,256]{0,1:T(8,128)} async-done(((f32[256,256]{0,1:T(8,128)}), f32[8192,256]{0,1:T(8,128)}) %all-gather.6.cloned.1.call-update) | async-done | bytes 8388624 | tf_op jit(solution)/shard_map/all_gather | solution.py:6
  431.6 6.8 %copy.15 = f32[32,8,32,256]{3,2,1,0:T(8,128)S(1)} copy(f32[32,8,32,256]{3,1,2,0:T(8,128)} %bitcast.91) | data formatting | bytes 16777216
  438.5 1.9 bitcast_reduce_fusion
  440.4 0.8 copy.13
  (25 shorter events, 0.2 us)
Async XLA Ops:
  7.2 1.0 copy-start
  7.2 56.7 %all-gather.4.cloned.1.call-start = ((), (), s32[]{:S(2)}) async-start(), calls=%async_computation.2 | async-start | bytes 4456448 | tf_op jit(solution)/shard_map/all_gather | solution.py:44
  10.0 149.2 %reduce-scatter.3.cloned.1.call-start = ((), (), s32[]{:S(2)}) async-start(), calls=%async_computation.3 | async-start | bytes 786432 | tf_op jit(solution)/shard_map/reduce_scatter | solution.py:58
  145.8 13.3 %copy-start.2 = (bf16[512,256]{1,0:T(8,128)(2,1)S(1)}, bf16[512,256]{1,0:T(8,128)(2,1)}, u32[]{:S(2)}) copy-start(bf16[512,256]{1,0:T(8,128)(2,1)} %param.12) | copy-start | bytes 786436
  145.8 199.4 %reduce-scatter.5.cloned.1.call-start = ((), (), s32[]{:S(2)}) async-start(), calls=%async_computation.4 | async-start | bytes 4456448 | tf_op jit(solution)/shard_map/reduce_scatter | solution.py:72
  266.4 80.7 %copy-start.1 = (bf16[256,256]{1,0:T(8,128)(2,1)S(1)}, bf16[256,256]{1,0:T(8,128)(2,1)}, u32[]{:S(2)}) copy-start(bf16[256,256]{1,0:T(8,128)(2,1)} %param.13) | copy-start | bytes 393220
  272.4 159.2 %all-gather.6.cloned.1.call-start = ((), (), s32[]{:S(2)}) async-start(), calls=%async_computation.5 | async-start | bytes 8650752 | tf_op jit(solution)/shard_map/all_gather | solution.py:6
Sparse Core Ops, SparseCore 0:
  10.7 53.0 all-gather.3
  145.9 13.1 reduce-scatter.2
  272.5 72.6 reduce-scatter.4
  348.5 83.0 all-gather.5
